TPU v7x, 32 devices: a whole 2x2x4 slice. The times are simulated.
32 devices in a mesh: row: 4 (over y, x), col: 8 (over z, core).
Axes of the slice: x: 2, y: 2, z: 4, core: 2. Of those that a mesh axis runs over, the one named last changes fastest.
Arguments:
- ancestor_inverse: float32 [24576, 24576], P('row', 'col'), may hold values from -0.0546875 to 0.0546875
- lower_panel: float32 [2, 24576, 256], P(None, ('row', 'col')), may hold values from -6 to 6
- diag_factor: float32 [2, 256, 256], replicated, may hold values from -0.09375 to 0.09375
- diag_block: float32 [2, 256, 256], replicated, may hold values from -24 to 24
- pattern: int32 [2, 384], replicated, may hold values 0 or 1
Outputs:
- panel_inverse: float32 [2, 24576, 256], P(None, ('row', 'col'))
- diag_inverse: float32 [2, 256, 256], replicated
All inputs are finite; a program needn't handle non-finite values.
Results may differ from a plain program's by a relative error of at most 0.000071.
Values sent between devices are 32-bit elements; how exact they have to be, the bound alone decides.
A program may use at most 192 MiB of HBM per device.

v0:
```python
import jax
import jax.numpy as jnp
from jax import lax
from jax.sharding import PartitionSpec as P

HIGHEST_PREC = lax.Precision.HIGHEST
HIGH_PREC = lax.Precision.HIGH


def local(ancestor_inverse, lower_panel, diag_factor, diag_block, pattern):
    row_count = lax.axis_size("row")
    col_count = lax.axis_size("col")
    row_index = lax.axis_index("row")
    col_index = lax.axis_index("col")
    snodes, piece_rows, width = lower_panel.shape
    tile_rows = row_count * col_count * piece_rows // pattern.shape[1]
    piece_start = (row_index * col_count + col_index) * piece_rows
    blocks = lax.dynamic_slice_in_dim(pattern, piece_start // tile_rows, piece_rows // tile_rows, 1)
    mask = jnp.repeat(blocks, tile_rows, axis=1).astype(jnp.float32)[:, :, None]
    normed = jnp.einsum("spw,swv->spv", lower_panel, diag_factor, precision=HIGHEST_PREC) * mask
    part_rows = piece_rows // row_count
    parts = normed.reshape(snodes, row_count, part_rows, width)
    number = (row_index * col_count + col_index) % row_count
    strips = []
    for snode in range(snodes):
        rounds = []
        for step in range(row_count):
            pairs = []
            for r in range(row_count):
                for c in range(col_count):
                    piece = r * col_count + c
                    q = (piece % row_count + step) % row_count
                    pairs.append((piece, q * col_count + piece // row_count))
            block = lax.dynamic_index_in_dim(parts[snode], (number + step) % row_count, 0, False)
            rounds.append(lax.ppermute(block, ("row", "col"), pairs))
        order = (row_index - jnp.arange(row_count)) % row_count
        received = jnp.take(jnp.stack(rounds), order, axis=0)
        everything = lax.all_gather(received, "row", axis=0)
        strips.append(jnp.swapaxes(everything, 0, 1).reshape(row_count * piece_rows, width))
    panels = []
    for snode in range(snodes):
        product = jnp.dot(ancestor_inverse, strips[snode], precision=HIGH_PREC)
        share = lax.psum_scatter(product, "col", scatter_dimension=0, tiled=True)
        panels.append(-share * mask[snode])
    panel_inverse = jnp.stack(panels)
    partial = jnp.einsum("spw,spv->swv", normed, panel_inverse, precision=HIGHEST_PREC)
    diag_inverse = diag_block - lax.psum(partial, ("row", "col"))
    return (panel_inverse, diag_inverse)


def solution(mesh):
    return jax.shard_map(
        local,
        mesh=mesh,
        in_specs=(P("row", "col"), P(None, ("row", "col"), None), P(), P(), P()),
        out_specs=(P(None, ("row", "col"), None), P()),
        check_vma=False,
    )
```

profile of v0, /device:TPU:0, one launch (start us, length us, event | category | flops | bytes accessed | tf_op | source)
XLA Modules:
  0.0 533.6 jit_solution(12290840376613704863)
XLA Ops:
  8.6 2.5 convolution_multiply_fusion
  11.1 1.2 fusion.3
  12.4 1.3 dynamic-slice_bitcast_fusion.3
  14.3 7.7 %collective-permute-start.5 = (f32[192,256]{1,0:T(8,128)S(1)}, f32[192,256]{1,0:T(8,128)S(1)}, u32[]{:S(2)}, u32[]{:S(2)}) collective-permute-start(f32[192,256]{1,0:T(8,128)S(1)} %get-tuple-element.20), channel_id=1, source_target_pairs={{0,8},{1,16},{2,24},{3,0},{4,9},{5,17},{6,25},{7,1},{8,10},{9,18},... | collective-permute-start | bytes 589832 | tf_op jit(solution)/shard_map/ppermute | solution.py:35
  22.0 2.0 collective-permute-start.6
  24.0 5.0 collective-permute-start.7
  29.0 2.0 dynamic-slice_bitcast_fusion.7
  31.0 3.0 collective-permute-start
  34.1 4.7 collective-permute-start.1
  38.7 45.7 %collective-permute-done.5 = f32[192,256]{1,0:T(8,128)S(1)} collective-permute-done((f32[192,256]{1,0:T(8,128)S(1)}, f32[192,256]{1,0:T(8,128)S(1)}, u32[]{:S(2)}, u32[]{:S(2)}) %collective-permute-start.5) | collective-permute-done | bytes 196640 | tf_op jit(solution)/shard_map/ppermute | solution.py:35
  84.5 16.8 %collective-permute-done.6 = f32[192,256]{1,0:T(8,128)S(1)} collective-permute-done((f32[192,256]{1,0:T(8,128)S(1)}, f32[192,256]{1,0:T(8,128)S(1)}, u32[]{:S(2)}, u32[]{:S(2)}) %collective-permute-start.6) | collective-permute-done | bytes 196640 | tf_op jit(solution)/shard_map/ppermute | solution.py:35
  101.3 1.9 collective-permute-start.3
  103.2 0.9 pad_maximum_fusion.2
  104.2 2.6 gather_fusion.1
  106.8 7.3 %collective-permute-done.1 = f32[192,256]{1,0:T(8,128)} collective-permute-done((f32[192,256]{1,0:T(8,128)}, f32[192,256]{1,0:T(8,128)}, u32[]{:S(2)}, u32[]{:S(2)}) %collective-permute-start.1) | collective-permute-done | bytes 196640 | tf_op jit(solution)/shard_map/ppermute | solution.py:35
  114.1 4.2 collective-permute-done.2
  118.2 2.1 pad_maximum_fusion.1
  120.4 2.7 gather_fusion
  123.1 2.8 broadcast_select_fusion.1
  126.7 46.5 %all-gather.5.cloned.1.call-done = f32[16,192,256]{2,1,0:T(8,128)} async-done(((f32[4,192,256]{2,1,0:T(8,128)}), f32[16,192,256]{2,1,0:T(8,128)}) %all-gather.5.cloned.1.call-update) | async-done | bytes 3145744 | tf_op jit(solution)/shard_map/all_gather | solution.py:38
  173.1 3.8 copy.18
  177.0 69.9 %convolution_bitcast_fusion.1 = f32[6144,256]{0,1:T(8,128)} fusion(f32[3072,256]{1,0:T(8,128)} %bitcast.53, f32[6144,3072]{1,0:T(8,128)} %param.7), kind=kOutput, calls=%fused_computation.3 | convolution fusion | flops 28991029248 | bytes 84934656 | tf_op jit(solution)/shard_map/dot_general | solution.py:42
  247.0 3.8 copy.19
  250.8 69.9 %convolution_bitcast_fusion = f32[6144,256]{0,1:T(8,128)} fusion(f32[3072,256]{1,0:T(8,128)} %bitcast.54, f32[6144,3072]{1,0:T(8,128)} %param.7), kind=kOutput, calls=%fused_computation.2 | convolution fusion | flops 28991029248 | bytes 84934656 | tf_op jit(solution)/shard_map/dot_general | solution.py:42
  321.0 2.1 multiply_bitcast_fusion.1
  323.1 67.4 %reduce-scatter.5.cloned.1.call-done = f32[768,256]{0,1:T(8,128)} async-done(((f32[6144,256]{0,1:T(8,128)}), f32[768,256]{0,1:T(8,128)}) %reduce-scatter.5.cloned.1.call-update) | async-done | bytes 786448 | tf_op jit(solution)/shard_map/reduce_scatter | solution.py:43
  390.6 1.2 multiply_bitcast_fusion
  392.6 4.6 fusion.2
  397.3 1.5 pad_maximum_fusion
  398.8 1.6 copy.22
  400.4 124.6 %all-reduce.2.cloned.1.call-done = f32[2,256,256]{2,1,0:T(8,128)} async-done(((f32[2,256,256]{2,1,0:T(8,128)}), f32[2,256,256]{2,1,0:T(8,128)}) %all-reduce.2.cloned.1.call-update) | async-done | bytes 524304 | tf_op jit(solution)/shard_map/psum | solution.py:47
  525.0 2.1 sub.18
  (33 shorter events, 4.1 us)
Async XLA Ops:
  7.2 1.4 copy-start
  7.2 166.0 %all-gather.5.cloned.1.call-start = ((), (), s32[]{:S(2)}) async-start(), calls=%async_computation.5 | async-start | bytes 3932160 | tf_op jit(solution)/shard_map/all_gather | solution.py:38
  13.7 20.4 %collective-permute-start.4 = (f32[192,256]{1,0:T(8,128)S(1)}, f32[192,256]{1,0:T(8,128)S(1)}, u32[]{:S(2)}, u32[]{:S(2)}) collective-permute-start(f32[192,256]{1,0:T(8,128)S(1)} %get-tuple-element.17), channel_id=1, source_target_pairs={{0,0},{1,8},{2,16},{3,24},{4,1},{5,9},{6,17},{7,25},{8,2},{9,10},{... | collective-permute-start | bytes 589832 | tf_op jit(solution)/shard_map/ppermute | solution.py:35
  14.3 70.1 %collective-permute-start.5 = (f32[192,256]{1,0:T(8,128)S(1)}, f32[192,256]{1,0:T(8,128)S(1)}, u32[]{:S(2)}, u32[]{:S(2)}) collective-permute-start(f32[192,256]{1,0:T(8,128)S(1)} %get-tuple-element.20), channel_id=1, source_target_pairs={{0,8},{1,16},{2,24},{3,0},{4,9},{5,17},{6,25},{7,1},{8,10},{9,18},... | collective-permute-start | bytes 589832 | tf_op jit(solution)/shard_map/ppermute | solution.py:35
  22.0 79.3 %collective-permute-start.6 = (f32[192,256]{1,0:T(8,128)S(1)}, f32[192,256]{1,0:T(8,128)S(1)}, u32[]{:S(2)}, u32[]{:S(2)}) collective-permute-start(f32[192,256]{1,0:T(8,128)S(1)} %get-tuple-element.19), channel_id=1, source_target_pairs={{0,16},{1,24},{2,0},{3,8},{4,17},{5,25},{6,1},{7,9},{8,18},{9,26},... | collective-permute-start | bytes 589832 | tf_op jit(solution)/shard_map/ppermute | solution.py:35
  24.0 79.2 %collective-permute-start.7 = (f32[192,256]{1,0:T(8,128)S(1)}, f32[192,256]{1,0:T(8,128)S(1)}, u32[]{:S(2)}, u32[]{:S(2)}) collective-permute-start(f32[192,256]{1,0:T(8,128)S(1)} %get-tuple-element.18), channel_id=1, source_target_pairs={{0,24},{1,0},{2,8},{3,16},{4,25},{5,1},{6,9},{7,17},{8,26},{9,2},{... | collective-permute-start | bytes 589832 | tf_op jit(solution)/shard_map/ppermute | solution.py:35
  31.0 75.7 %collective-permute-start = (f32[192,256]{1,0:T(8,128)}, f32[192,256]{1,0:T(8,128)}, u32[]{:S(2)}, u32[]{:S(2)}) collective-permute-start(f32[192,256]{1,0:T(8,128)} %get-tuple-element.13), channel_id=1, source_target_pairs={{0,0},{1,8},{2,16},{3,24},{4,1},{5,9},{6,17},{7,25},{8,2},{9,10},{... | collective-permute-start | bytes 589832 | tf_op jit(solution)/shard_map/ppermute | solution.py:35
  34.1 80.0 %collective-permute-start.1 = (f32[192,256]{1,0:T(8,128)}, f32[192,256]{1,0:T(8,128)}, u32[]{:S(2)}, u32[]{:S(2)}) collective-permute-start(f32[192,256]{1,0:T(8,128)} %get-tuple-element.16), channel_id=1, source_target_pairs={{0,8},{1,16},{2,24},{3,0},{4,9},{5,17},{6,25},{7,1},{8,10},{9,18},... | collective-permute-start | bytes 589832 | tf_op jit(solution)/shard_map/ppermute | solution.py:35
  84.5 33.8 %collective-permute-start.2 = (f32[192,256]{1,0:T(8,128)S(1)}, f32[192,256]{1,0:T(8,128)}, u32[]{:S(2)}, u32[]{:S(2)}) collective-permute-start(f32[192,256]{1,0:T(8,128)S(1)} %get-tuple-element.15), channel_id=1, source_target_pairs={{0,16},{1,24},{2,0},{3,8},{4,17},{5,25},{6,1},{7,9},{8,18},{9,26},... | collective-permute-start | bytes 589832 | tf_op jit(solution)/shard_map/ppermute | solution.py:35
  101.3 17.0 %collective-permute-start.3 = (f32[192,256]{1,0:T(8,128)S(1)}, f32[192,256]{1,0:T(8,128)}, u32[]{:S(2)}, u32[]{:S(2)}) collective-permute-start(f32[192,256]{1,0:T(8,128)S(1)} %get-tuple-element.14), channel_id=1, source_target_pairs={{0,24},{1,0},{2,8},{3,16},{4,25},{5,1},{6,9},{7,17},{8,26},{9,2},{... | collective-permute-start | bytes 589832 | tf_op jit(solution)/shard_map/ppermute | solution.py:35
  125.9 121.1 %all-gather.7.cloned.1.call-start = ((), (), s32[]{:S(2)}) async-start(), calls=%async_computation.6 | async-start | bytes 3932160 | tf_op jit(solution)/shard_map/all_gather | solution.py:38
  126.6 194.4 %reduce-scatter.3.cloned.1.call-start = ((), (), s32[]{:S(2)}) async-start(), calls=%async_computation.2 | async-start | bytes 7077888 | tf_op jit(solution)/shard_map/reduce_scatter | solution.py:43
  246.9 143.7 %reduce-scatter.5.cloned.1.call-start = ((), (), s32[]{:S(2)}) async-start(), calls=%async_computation.3 | async-start | bytes 7077888 | tf_op jit(solution)/shard_map/reduce_scatter | solution.py:43
  320.7 204.3 %all-reduce.2.cloned.1.call-start = ((), (), s32[]{:S(2)}) async-start(), calls=%async_computation.4 | async-start | bytes 1048576 | tf_op jit(solution)/shard_map/psum | solution.py:47
  391.8 0.9 copy-start.1
Sparse Core Ops, SparseCore 0:
  126.0 47.1 all-gather.4
  175.0 43.8 all-gather.6
  247.0 69.6 reduce-scatter.2
  320.8 69.7 reduce-scatter.4
  397.4 127.5 all-reduce.1
where the time goes:
time: 534 us
  waiting for transfers between devices  313 us (59%)
  matrix products  147 us (28%)
  starting transfers between devices  25.1 us (5%)
  local copies, waits for them, and re-layouts  20.7 us (4%)
  between operations  14 us (3%)
  other arithmetic  13.6 us (3%)
    dot_general x2, matrix products, local(): product = jnp.dot(ancestor_inverse, strips[snode], precision=HIGH_PREC)  140 us
    psum x1, waiting for transfers between devices, local(): diag_inverse = diag_block - lax.psum(partial, ('row', 'col'))  125 us
    ppermute x8, waiting for transfers between devices, local(): rounds.append(lax.ppermute(block, ('row', 'col'), pairs))  74 us
    reduce_scatter x2, waiting for transfers between devices, local(): share = lax.psum_scatter(product, 'col', scatter_dimension=0, tiled=True)  67.4 us
    all_gather x2, waiting for transfers between devices, local(): everything = lax.all_gather(received, 'row', axis=0)  46.5 us
    ppermute x8, starting transfers between devices, local(): rounds.append(lax.ppermute(block, ('row', 'col'), pairs))  24.9 us
  transfers between devices with their start and end apart: 13, of which 7 were waited for; matrix products, arithmetic and copies ran while one was open for 30% of the time, Pallas kernels for 0%

commit v1 on v0

--- a/solution.py
+++ b/solution.py
@@ -44,7 +44,7 @@
         panels.append(-share * mask[snode])
     panel_inverse = jnp.stack(panels)
     partial = jnp.einsum("spw,spv->swv", normed, panel_inverse, precision=HIGHEST_PREC)
-    diag_inverse = diag_block - lax.psum(partial, ("row", "col"))
+    diag_inverse = diag_block - lax.psum(lax.psum(partial, "row"), "col")
     return (panel_inverse, diag_inverse)
 
 

time: 534 us -> 510 us (0.955)
  waiting for transfers between devices: 313 us -> 288 us
    psum x1 -> x2, waiting for transfers between devices: 125 us -> 99.5 us  [local(): diag_inverse = diag_block - lax.psum(lax.psum(partial, 'row'), 'col')]
  transfers between devices with their start and end apart: 13 -> 14, of which waited for: 7 -> 8; matrix products, arithmetic and copies ran while one was open for 30% -> 31% of each run, Pallas kernels for 0% -> 0%
where the time goes in v1:
time: 510 us; the launch traced here: 509 us
  waiting for transfers between devices  288 us (56%)
  matrix products  147 us (29%)
  starting transfers between devices  25.1 us (5%)
  local copies, waits for them, and re-layouts  20.7 us (4%)
  between operations  14.3 us (3%)
  other arithmetic  13.6 us (3%)
    dot_general x2, matrix products, local(): product = jnp.dot(ancestor_inverse, strips[snode], precision=HIGH_PREC)  140 us
    psum x2, waiting for transfers between devices, local(): diag_inverse = diag_block - lax.psum(lax.psum(partial, 'row'), 'col')  99.5 us
    ppermute x8, waiting for transfers between devices, local(): rounds.append(lax.ppermute(block, ('row', 'col'), pairs))  74 us
    reduce_scatter x2, waiting for transfers between devices, local(): share = lax.psum_scatter(product, 'col', scatter_dimension=0, tiled=True)  67.4 us
    all_gather x2, waiting for transfers between devices, local(): everything = lax.all_gather(received, 'row', axis=0)  46.5 us
    ppermute x8, starting transfers between devices, local(): rounds.append(lax.ppermute(block, ('row', 'col'), pairs))  24.9 us
  transfers between devices with their start and end apart: 14, of which 8 were waited for; matrix products, arithmetic and copies ran while one was open for 31% of the time, Pallas kernels for 0%

profile of v1, /device:TPU:0, one launch (start us, length us, event | category | flops | bytes accessed | tf_op | source)
XLA Modules:
  0.0 508.9 jit_solution(10404822289834848666)
XLA Ops:
  8.6 2.5 convolution_multiply_fusion
  11.1 1.2 fusion.3
  12.4 1.3 dynamic-slice_bitcast_fusion.3
  14.3 7.7 %collective-permute-start.5 = (f32[192,256]{1,0:T(8,128)S(1)}, f32[192,256]{1,0:T(8,128)S(1)}, u32[]{:S(2)}, u32[]{:S(2)}) collective-permute-start(f32[192,256]{1,0:T(8,128)S(1)} %get-tuple-element.20), channel_id=1, source_target_pairs={{0,8},{1,16},{2,24},{3,0},{4,9},{5,17},{6,25},{7,1},{8,10},{9,18},... | collective-permute-start | bytes 589832 | tf_op jit(solution)/shard_map/ppermute | solution.py:35
  22.0 2.0 collective-permute-start.6
  24.0 5.0 collective-permute-start.7
  29.0 2.0 dynamic-slice_bitcast_fusion.7
  31.0 3.0 collective-permute-start
  34.1 4.7 collective-permute-start.1
  38.7 45.7 %collective-permute-done.5 = f32[192,256]{1,0:T(8,128)S(1)} collective-permute-done((f32[192,256]{1,0:T(8,128)S(1)}, f32[192,256]{1,0:T(8,128)S(1)}, u32[]{:S(2)}, u32[]{:S(2)}) %collective-permute-start.5) | collective-permute-done | bytes 196640 | tf_op jit(solution)/shard_map/ppermute | solution.py:35
  84.5 16.8 %collective-permute-done.6 = f32[192,256]{1,0:T(8,128)S(1)} collective-permute-done((f32[192,256]{1,0:T(8,128)S(1)}, f32[192,256]{1,0:T(8,128)S(1)}, u32[]{:S(2)}, u32[]{:S(2)}) %collective-permute-start.6) | collective-permute-done | bytes 196640 | tf_op jit(solution)/shard_map/ppermute | solution.py:35
  101.3 1.9 collective-permute-start.3
  104.2 2.6 gather_fusion.1
  106.8 7.3 %collective-permute-done.1 = f32[192,256]{1,0:T(8,128)} collective-permute-done((f32[192,256]{1,0:T(8,128)}, f32[192,256]{1,0:T(8,128)}, u32[]{:S(2)}, u32[]{:S(2)}) %collective-permute-start.1) | collective-permute-done | bytes 196640 | tf_op jit(solution)/shard_map/ppermute | solution.py:35
  114.1 4.2 collective-permute-done.2
  118.2 2.1 pad_maximum_fusion.1
  120.4 2.7 gather_fusion
  123.1 2.8 broadcast_select_fusion.1
  126.7 46.5 %all-gather.5.cloned.1.call-done = f32[16,192,256]{2,1,0:T(8,128)} async-done(((f32[4,192,256]{2,1,0:T(8,128)}), f32[16,192,256]{2,1,0:T(8,128)}) %all-gather.5.cloned.1.call-update) | async-done | bytes 3145744 | tf_op jit(solution)/shard_map/all_gather | solution.py:38
  173.1 3.8 copy.18
  177.0 69.9 %convolution_bitcast_fusion.1 = f32[6144,256]{0,1:T(8,128)} fusion(f32[3072,256]{1,0:T(8,128)} %bitcast.53, f32[6144,3072]{1,0:T(8,128)} %param.7), kind=kOutput, calls=%fused_computation.3 | convolution fusion | flops 28991029248 | bytes 84934656 | tf_op jit(solution)/shard_map/dot_general | solution.py:42
  247.0 3.8 copy.19
  250.8 69.9 %convolution_bitcast_fusion = f32[6144,256]{0,1:T(8,128)} fusion(f32[3072,256]{1,0:T(8,128)} %bitcast.54, f32[6144,3072]{1,0:T(8,128)} %param.7), kind=kOutput, calls=%fused_computation.2 | convolution fusion | flops 28991029248 | bytes 84934656 | tf_op jit(solution)/shard_map/dot_general | solution.py:42
  321.0 2.1 multiply_bitcast_fusion.1
  323.2 67.4 %reduce-scatter.5.cloned.1.call-done = f32[768,256]{0,1:T(8,128)} async-done(((f32[6144,256]{0,1:T(8,128)}), f32[768,256]{0,1:T(8,128)}) %reduce-scatter.5.cloned.1.call-update) | async-done | bytes 786448 | tf_op jit(solution)/shard_map/reduce_scatter | solution.py:43
  390.6 1.2 multiply_bitcast_fusion
  392.6 4.6 fusion.2
  397.4 43.9 %all-reduce.3.cloned.1.call-done = f32[2,256,256]{2,1,0:T(8,128)} async-done(((f32[2,256,256]{2,1,0:T(8,128)}), f32[2,256,256]{2,1,0:T(8,128)}) %all-reduce.3.cloned.1.call-update) | async-done | bytes 524304 | tf_op jit(solution)/shard_map/psum | solution.py:47
  441.3 1.5 pad_maximum_fusion
  442.8 1.6 copy.22
  444.4 55.6 %all-reduce.5.cloned.1.call-done = f32[2,256,256]{2,1,0:T(8,128)} async-done(((f32[2,256,256]{2,1,0:T(8,128)}), f32[2,256,256]{2,1,0:T(8,128)}) %all-reduce.5.cloned.1.call-update) | async-done | bytes 524304 | tf_op jit(solution)/shard_map/psum | solution.py:47
  500.0 2.1 sub.18
  (36 shorter events, 5.1 us)
Async XLA Ops:
  7.2 1.4 copy-start
  7.2 166.0 %all-gather.5.cloned.1.call-start = ((), (), s32[]{:S(2)}) async-start(), calls=%async_computation.6 | async-start | bytes 3932160 | tf_op jit(solution)/shard_map/all_gather | solution.py:38
  13.7 20.4 %collective-permute-start.4 = (f32[192,256]{1,0:T(8,128)S(1)}, f32[192,256]{1,0:T(8,128)S(1)}, u32[]{:S(2)}, u32[]{:S(2)}) collective-permute-start(f32[192,256]{1,0:T(8,128)S(1)} %get-tuple-element.17), channel_id=1, source_target_pairs={{0,0},{1,8},{2,16},{3,24},{4,1},{5,9},{6,17},{7,25},{8,2},{9,10},{... | collective-permute-start | bytes 589832 | tf_op jit(solution)/shard_map/ppermute | solution.py:35
  14.3 70.1 %collective-permute-start.5 = (f32[192,256]{1,0:T(8,128)S(1)}, f32[192,256]{1,0:T(8,128)S(1)}, u32[]{:S(2)}, u32[]{:S(2)}) collective-permute-start(f32[192,256]{1,0:T(8,128)S(1)} %get-tuple-element.20), channel_id=1, source_target_pairs={{0,8},{1,16},{2,24},{3,0},{4,9},{5,17},{6,25},{7,1},{8,10},{9,18},... | collective-permute-start | bytes 589832 | tf_op jit(solution)/shard_map/ppermute | solution.py:35
  22.0 79.3 %collective-permute-start.6 = (f32[192,256]{1,0:T(8,128)S(1)}, f32[192,256]{1,0:T(8,128)S(1)}, u32[]{:S(2)}, u32[]{:S(2)}) collective-permute-start(f32[192,256]{1,0:T(8,128)S(1)} %get-tuple-element.19), channel_id=1, source_target_pairs={{0,16},{1,24},{2,0},{3,8},{4,17},{5,25},{6,1},{7,9},{8,18},{9,26},... | collective-permute-start | bytes 589832 | tf_op jit(solution)/shard_map/ppermute | solution.py:35
  24.0 79.2 %collective-permute-start.7 = (f32[192,256]{1,0:T(8,128)S(1)}, f32[192,256]{1,0:T(8,128)S(1)}, u32[]{:S(2)}, u32[]{:S(2)}) collective-permute-start(f32[192,256]{1,0:T(8,128)S(1)} %get-tuple-element.18), channel_id=1, source_target_pairs={{0,24},{1,0},{2,8},{3,16},{4,25},{5,1},{6,9},{7,17},{8,26},{9,2},{... | collective-permute-start | bytes 589832 | tf_op jit(solution)/shard_map/ppermute | solution.py:35
  31.0 75.7 %collective-permute-start = (f32[192,256]{1,0:T(8,128)}, f32[192,256]{1,0:T(8,128)}, u32[]{:S(2)}, u32[]{:S(2)}) collective-permute-start(f32[192,256]{1,0:T(8,128)} %get-tuple-element.13), channel_id=1, source_target_pairs={{0,0},{1,8},{2,16},{3,24},{4,1},{5,9},{6,17},{7,25},{8,2},{9,10},{... | collective-permute-start | bytes 589832 | tf_op jit(solution)/shard_map/ppermute | solution.py:35
  34.1 80.0 %collective-permute-start.1 = (f32[192,256]{1,0:T(8,128)}, f32[192,256]{1,0:T(8,128)}, u32[]{:S(2)}, u32[]{:S(2)}) collective-permute-start(f32[192,256]{1,0:T(8,128)} %get-tuple-element.16), channel_id=1, source_target_pairs={{0,8},{1,16},{2,24},{3,0},{4,9},{5,17},{6,25},{7,1},{8,10},{9,18},... | collective-permute-start | bytes 589832 | tf_op jit(solution)/shard_map/ppermute | solution.py:35
  84.5 33.8 %collective-permute-start.2 = (f32[192,256]{1,0:T(8,128)S(1)}, f32[192,256]{1,0:T(8,128)}, u32[]{:S(2)}, u32[]{:S(2)}) collective-permute-start(f32[192,256]{1,0:T(8,128)S(1)} %get-tuple-element.15), channel_id=1, source_target_pairs={{0,16},{1,24},{2,0},{3,8},{4,17},{5,25},{6,1},{7,9},{8,18},{9,26},... | collective-permute-start | bytes 589832 | tf_op jit(solution)/shard_map/ppermute | solution.py:35
  101.3 17.0 %collective-permute-start.3 = (f32[192,256]{1,0:T(8,128)S(1)}, f32[192,256]{1,0:T(8,128)}, u32[]{:S(2)}, u32[]{:S(2)}) collective-permute-start(f32[192,256]{1,0:T(8,128)S(1)} %get-tuple-element.14), channel_id=1, source_target_pairs={{0,24},{1,0},{2,8},{3,16},{4,25},{5,1},{6,9},{7,17},{8,26},{9,2},{... | collective-permute-start | bytes 589832 | tf_op jit(solution)/shard_map/ppermute | solution.py:35
  125.9 121.1 %all-gather.7.cloned.1.call-start = ((), (), s32[]{:S(2)}) async-start(), calls=%async_computation.7 | async-start | bytes 3932160 | tf_op jit(solution)/shard_map/all_gather | solution.py:38
  126.6 194.4 %reduce-scatter.3.cloned.1.call-start = ((), (), s32[]{:S(2)}) async-start(), calls=%async_computation.2 | async-start | bytes 7077888 | tf_op jit(solution)/shard_map/reduce_scatter | solution.py:43
  246.9 143.7 %reduce-scatter.5.cloned.1.call-start = ((), (), s32[]{:S(2)}) async-start(), calls=%async_computation.3 | async-start | bytes 7077888 | tf_op jit(solution)/shard_map/reduce_scatter | solution.py:43
  320.7 120.6 %all-reduce.3.cloned.1.call-start = ((), (), s32[]{:S(2)}) async-start(), calls=%async_computation.4 | async-start | bytes 1048576 | tf_op jit(solution)/shard_map/psum | solution.py:47
  391.8 0.9 copy-start.1
  397.3 102.7 %all-reduce.5.cloned.1.call-start = ((), (), s32[]{:S(2)}) async-start(), calls=%async_computation.5 | async-start | bytes 1048576 | tf_op jit(solution)/shard_map/psum | solution.py:47
Sparse Core Ops, SparseCore 0:
  126.0 47.1 all-gather.4
  175.0 43.8 all-gather.6
  247.0 69.6 reduce-scatter.2
  320.8 69.7 reduce-scatter.4
  397.4 43.8 all-reduce.2
  443.5 56.4 all-reduce.4
